TPU v7x, 128 devices: a whole 4x4x4 slice. The times are simulated.
128 devices in a mesh: tm: 32 (over x, z, core), panel: 4 (over y).
Axes of the slice: x: 4, y: 4, z: 4, core: 2. Of those that a mesh axis runs over, the one named last changes fastest.
Arguments:
- design: bfloat16 [8192, 7680], P('tm', 'panel'), may hold values from -6 to 6
- partials: bfloat16 [8192, 64], P('tm'), may hold values from -0.119628906 to 0.119628906
- observed: bfloat16 [8192], P('tm'), may hold values from -6 to 6
- arc_of_row: int32 [8192, 1], replicated, may hold values from 0 to 31, as said below
- autoreg: float32 [32], replicated, may hold values from -0.55 to 0.5
- movavg: float32 [32], replicated, may hold values from 0.3 to 0.9
Outputs:
- normal: float32 [7680, 7680], P('tm', 'panel')
- right_hand: float32 [7680], P('panel')
Inputs may be any that keep to these rules, and one draw needn't show every extreme that they name: arc_of_row never falls along the epochs and names every arc; arcs 2b and 2b + 1 together have 2 * 256 epochs, one of them 384 // 3 to 160 epochs and the other 352 to 384; one arc has exactly 384 epochs and its partner exactly 128, so that at most 12 rows of one device belong to one arc, and every device holds exactly 12 rows of the longest arc; arc a is held by index a of tm.
All inputs are finite; a program needn't handle non-finite values.
Results may differ from a plain program's by a relative error of at most 0.02.
Values may be sent and summed in bfloat16 or wider, within the bound.
A program may use at most 192 MiB of HBM per device.

v0:
```python
import jax
import jax.numpy as jnp
from jax import lax
from jax.sharding import PartitionSpec as P


def whiten_matrix(order_row, order_col, usable_row, usable_col, ar_value, ma_value):
    spacing = order_row[:, None] - order_col[None, :]
    lag_steps = jnp.maximum(spacing - 1, 0)
    parity = (lag_steps % 2).astype(jnp.float32)
    flip_sign = 1.0 - 2.0 * parity
    decayed = (
        -(ar_value + ma_value)
        * flip_sign
        * jnp.exp(lag_steps.astype(jnp.float32) * jnp.log(ma_value))
    )
    entry = jnp.where(spacing == 0, jnp.float32(1.0), decayed)
    allowed = usable_row[:, None] & usable_col[None, :] & (spacing >= 0)
    return jnp.where(allowed, entry, jnp.float32(0.0)).astype(jnp.bfloat16)


def eliminate(whitener, rows_design, rows_params, rows_obs, scale):
    white_design = jnp.dot(whitener, rows_design, preferred_element_type=jnp.float32)
    white_params = jnp.dot(whitener, rows_params, preferred_element_type=jnp.float32)
    white_obs = jnp.dot(whitener, rows_obs, preferred_element_type=jnp.float32)
    param_count = rows_params.shape[1]
    param_gram = jnp.dot(white_params.T, white_params, precision=lax.Precision.HIGHEST) + jnp.eye(
        param_count, dtype=jnp.float32
    )
    factor = jnp.linalg.cholesky(param_gram)
    basis = lax.linalg.triangular_solve(factor, white_params.T, left_side=True, lower=True)
    arc_terms = jnp.dot(basis, white_design, precision=lax.Precision.HIGHEST)
    arc_rhs = jnp.dot(basis, white_obs, precision=lax.Precision.HIGHEST)
    right_part = (
        jnp.dot(white_design.T, white_obs, precision=lax.Precision.HIGHEST)
        - jnp.dot(arc_terms.T, arc_rhs, precision=lax.Precision.HIGHEST)
    ) * scale
    return (white_design.astype(jnp.bfloat16), arc_terms.astype(jnp.bfloat16), right_part)


def body(design, partials, observed, arc_of_row, autoreg, movavg):
    tile_count = lax.axis_size("tm")
    device_index = lax.axis_index("tm")
    rows_dev = design.shape[0]
    panel_width = design.shape[1]
    param_count = partials.shape[1]
    capacity = 3 * rows_dev // 2 // tile_count
    slot_count = tile_count * capacity
    scale = 1.0 / (rows_dev * tile_count)
    arc_ids = arc_of_row[:, 0]
    epoch_table = arc_ids.reshape(rows_dev, tile_count)
    local_arcs = lax.dynamic_slice_in_dim(epoch_table, device_index, 1, 1)[:, 0]
    onehot = (local_arcs[:, None] == jnp.arange(tile_count, dtype=jnp.int32)[None, :]).astype(
        jnp.int32
    )
    earlier = jnp.cumsum(onehot, axis=0) - onehot
    within = jnp.sum(earlier * onehot, axis=1)
    target_slot = local_arcs * capacity + within
    source_row = (
        jnp.zeros((slot_count,), jnp.int32)
        .at[target_slot]
        .set(jnp.arange(1, rows_dev + 1, dtype=jnp.int32))
    )

    def pick_rows(values):
        padded = jnp.concatenate([jnp.zeros((1,) + values.shape[1:], values.dtype), values], axis=0)
        return jnp.take(padded, source_row, axis=0)

    send_design = pick_rows(design).reshape(tile_count, capacity, panel_width)
    send_params = pick_rows(partials).reshape(tile_count, capacity, param_count)
    send_obs = pick_rows(observed).reshape(tile_count, capacity)
    got_design, got_params, got_obs = (
        lax.all_to_all(send_design, "tm", split_axis=0, concat_axis=0, tiled=True),
        lax.all_to_all(send_params, "tm", split_axis=0, concat_axis=0, tiled=True),
        lax.all_to_all(send_obs, "tm", split_axis=0, concat_axis=0, tiled=True),
    )
    got_design = got_design.reshape(slot_count, panel_width)
    got_params = got_params.reshape(slot_count, param_count)
    got_obs = got_obs.reshape(slot_count)
    per_source = jnp.sum((epoch_table == device_index).astype(jnp.int32), axis=0)
    arc_start = jnp.sum((arc_ids < device_index).astype(jnp.int32))
    first_pos = jnp.mod(jnp.arange(tile_count, dtype=jnp.int32) - arc_start, tile_count)
    offset_in = jnp.arange(capacity, dtype=jnp.int32)
    order_pos = (first_pos[:, None] + offset_in[None, :] * tile_count).reshape(slot_count)
    usable = (offset_in[None, :] < per_source[:, None]).reshape(slot_count)
    whitener = whiten_matrix(
        order_pos, order_pos, usable, usable, autoreg[device_index], movavg[device_index]
    )
    design_bf, terms_bf, right_part = eliminate(whitener, got_design, got_params, got_obs, scale)
    right_hand = lax.psum(right_part, "tm")
    own_rows = jnp.concatenate([design_bf, terms_bf], axis=0)
    signed_rows = jnp.concatenate([design_bf, -terms_bf], axis=0)
    gathered = lax.all_gather(signed_rows, "panel", axis=1, tiled=True)
    product = lax.dot_general(
        gathered, own_rows, (((0,), (0,)), ((), ())), preferred_element_type=jnp.float32
    )
    normal = lax.psum_scatter(
        (product * scale).astype(jnp.bfloat16), "tm", scatter_dimension=0, tiled=True
    ).astype(jnp.float32)
    return (normal, right_hand)


def solution(mesh):
    in_specs = (P("tm", "panel"), P("tm", None), P("tm"), P(), P(), P())
    out_specs = (P("tm", "panel"), P("panel"))
    return jax.shard_map(body, mesh=mesh, in_specs=in_specs, out_specs=out_specs, check_vma=False)
```

profile of v0, /device:TPU:1, one launch (start us, length us, event | category | flops | bytes accessed | tf_op | source)
XLA Modules:
  0.0 332.8 jit_solution(6460968665628124426)
XLA Ops:
  7.2 1.0 copy.16
  8.1 0.5 broadcast.193
  8.7 2.1 fusion.33
  10.8 0.1 reshape_squeeze.3
  10.9 0.0 copy-start.1
  10.9 0.2 dynamic-slice_reduce_fusion
  11.1 0.6 reduce-window.6
  11.7 0.2 slice_reduce_fusion
  11.9 0.1 fusion.36
  12.0 0.1 copy.15
  12.2 0.2 fusion.31
  12.4 1.4 scatter_custom_fusion
  13.8 0.7 pad_maximum_fusion.1
  14.5 2.8 gather_fusion.2
  17.4 0.1 broadcast_in_dim.54
  17.5 1.4 gather_fusion.1
  19.0 0.1 broadcast_select_fusion.1
  19.2 0.8 reshape.233
  19.9 9.4 %all-to-all-start.1 = ((bf16[32,2,384]{2,1,0:T(2,128)(2,1)}), bf16[32,2,384]{2,1,0:T(2,128)(2,1)S(1)}, u32[]{:S(2)}, u32[]{:S(2)}) async-start(bf16[32,2,384]{2,1,0:T(2,128)(2,1)} %reshape.233), calls=%async_computation.1 | async-start | bytes 98304 | tf_op jit(solution)/shard_map/all_to_all | solution.py:74
  29.4 0.7 and_select_fusion
  30.0 0.2 concatenate.15
  30.3 2.5 gather_fusion
  32.8 0.4 gather.17
  33.2 1.6 broadcast_select_fusion
  34.7 0.1 broadcast_add_fusion
  34.8 0.1 convert_reduce_fusion
  34.9 1.8 all-to-all-done.1
  36.7 5.6 %all-to-all-start = ((bf16[32,12,1920]{2,1,0:T(8,128)(2,1)}), bf16[32,12,1920]{2,1,0:T(8,128)(2,1)S(1)}, u32[]{:S(2)}, u32[]{:S(2)}) async-start(bf16[32,12,1920]{2,1,0:T(8,128)(2,1)} %broadcast_select_fusion), calls=%async_computation | async-start | bytes 3932160 | tf_op jit(solution)/shard_map/all_to_all | solution.py:73
  42.3 0.2 all-gather.2.cloned.1.call-start
  42.5 0.1 iota_compare_fusion.5
  42.6 0.6 dynamic_slice.10
  43.9 0.6 dynamic_slice.9
  45.8 0.1 add.112
  45.9 0.1 lt.72
  46.0 0.1 reshape.234
  46.2 0.7 fusion.27
  46.9 0.2 fusion.69
  47.2 0.1 copy.17
  47.3 5.8 %cholesky.17 = f32[64,64]{1,0:T(8,128)S(1)} custom-call(f32[64,64]{1,0:T(8,128)S(1)} %fusion.40), custom_call_target="Cholesky" | custom-call | tf_op jit(solution)/shard_map/jit(cholesky)/cholesky | solution.py:30
  53.2 0.6 compare_reduce_fusion
  53.8 0.7 fusion.32
  54.5 4.9 %custom-call.6 = f32[1,64,64]{1,2,0:T(8,128)S(1)} custom-call(f32[1,64,64]{2,1,0:T(8,128)S(1)} %fusion.32), custom_call_target="InvertDiagBlocksLowerTriangular" | custom-call | tf_op jit(solution)/shard_map/triangular_solve | solution.py:31
  59.4 0.3 fusion.37
  59.7 9.5 %all-to-all-done = bf16[32,12,1920]{2,1,0:T(8,128)(2,1)S(1)} async-done(((bf16[32,12,1920]{2,1,0:T(8,128)(2,1)}), bf16[32,12,1920]{2,1,0:T(8,128)(2,1)S(1)}, u32[]{:S(2)}, u32[]{:S(2)}) %all-to-all-start) | async-done | bytes 1474592 | tf_op jit(solution)/shard_map/all_to_all | solution.py:73
  69.2 1.3 reshape.165
  70.5 2.7 fusion.68
  73.2 2.3 fusion.67
  75.6 1.3 pad_maximum_fusion
  76.9 0.0 all-gather.2.cloned.1.call-update
  76.9 0.0 reduce-scatter.4.cloned.1.call-start
  76.9 68.3 %all-gather.2.cloned.1.call-done = bf16[448,7680]{1,0:T(8,128)(2,1)} async-done(((bf16[448,1920]{1,0:T(8,128)(2,1)}), bf16[448,7680]{1,0:T(8,128)(2,1)}) %all-gather.2.cloned.1.call-update) | async-done | bytes 6881296 | tf_op jit(solution)/shard_map/all_gather | solution.py:93
  145.3 22.9 %multiply_convert_fusion = bf16[7680,1920]{1,0:T(8,128)(2,1)} fusion(bf16[448,7680]{1,0:T(8,128)(2,1)} %all-gather.2.cloned.1.call-done, bf16[64,1920]{1,0:T(8,128)(2,1)} %get-tuple-element.7, bf16[384,1920]{1,0:T(8,128)(2,1)} %copy-done), kind=kOutput, calls=%fused_computation.4 | convolution fusion | flops 13244989440 | bytes 38092800 | tf_op jit(solution)/shard_map/dot_general | solution.py:94
  168.1 0.0 reduce-scatter.4.cloned.1.call-update
  168.2 0.7 select_n.84
  168.9 14.5 %all_to_all.16 = bf16[32,1,12]{2,1,0:T(2,128)(2,1)S(1)} all-to-all(bf16[32,1,12]{2,1,0:T(2,128)(2,1)} %select_n.84), channel_id=1, replica_groups=mesh['tm'=32,'panel'=4] {'tm'}, dimensions={0} | all-to-all | bytes 1536 | tf_op jit(solution)/shard_map/all_to_all | solution.py:75
  183.4 0.7 reduce.12
  184.1 0.8 reshape.203
  184.9 1.5 convolution_bitcast_fusion
  186.3 0.2 convolution_bitcast_fusion.1
  186.5 0.4 convolution_reduce_fusion
  187.0 1.7 fusion.5
  188.7 65.3 %psum.7 = f32[1920]{0:T(1024)} all-reduce(f32[1920]{0:T(1024)S(1)} %subtract_multiply_fusion), channel_id=1, replica_groups=mesh['tm'=32,'panel'=4] {'tm'}, use_global_device_ids=true, to_apply=%region_9.10 | all-reduce | flops 1920 | bytes 15360 | tf_op jit(solution)/shard_map/psum | solution.py:90
  254.0 69.5 %reduce-scatter.4.cloned.1.call-done = bf16[240,1920]{1,0:T(8,128)(2,1)} async-done(((bf16[7680,1920]{1,0:T(8,128)(2,1)}), bf16[240,1920]{1,0:T(8,128)(2,1)}) %reduce-scatter.4.cloned.1.call-update) | async-done | bytes 921616
  323.4 2.5 convert_element_type.57
  (29 shorter events, 0.3 us)
Async XLA Ops:
  7.2 22.9 %copy-start.3 = (bf16[256,1920]{1,0:T(8,128)(2,1)S(1)}, bf16[256,1920]{1,0:T(8,128)(2,1)}, u32[]{:S(2)}) copy-start(bf16[256,1920]{1,0:T(8,128)(2,1)} %param.6) | copy-start | bytes 2949124
  10.9 2.9 copy-start.1
  19.9 16.7 %all-to-all-start.1 = ((bf16[32,2,384]{2,1,0:T(2,128)(2,1)}), bf16[32,2,384]{2,1,0:T(2,128)(2,1)S(1)}, u32[]{:S(2)}, u32[]{:S(2)}) async-start(bf16[32,2,384]{2,1,0:T(2,128)(2,1)} %reshape.233), calls=%async_computation.1 | async-start | bytes 98304 | tf_op jit(solution)/shard_map/all_to_all | solution.py:74
  33.2 1.7 copy-start.2
  34.9 7.7 %copy-start.6 = (f32[32]{0:T(128)S(1)}, f32[32]{0:T(128)}, u32[]{:S(2)}) copy-start(f32[32]{0:T(128)} %param.11) | copy-start | bytes 388
  34.9 9.0 %copy-start.7 = (f32[32]{0:T(128)S(1)}, f32[32]{0:T(128)}, u32[]{:S(2)}) copy-start(f32[32]{0:T(128)} %param.10) | copy-start | bytes 388
  36.7 32.5 %all-to-all-start = ((bf16[32,12,1920]{2,1,0:T(8,128)(2,1)}), bf16[32,12,1920]{2,1,0:T(8,128)(2,1)S(1)}, u32[]{:S(2)}, u32[]{:S(2)}) async-start(bf16[32,12,1920]{2,1,0:T(8,128)(2,1)} %broadcast_select_fusion), calls=%async_computation | async-start | bytes 3932160 | tf_op jit(solution)/shard_map/all_to_all | solution.py:73
  42.3 103.0 %all-gather.2.cloned.1.call-start = ((), (), s32[]{:S(2)}) async-start(), calls=%async_computation.4 | async-start | bytes 8601600 | tf_op jit(solution)/shard_map/all_gather | solution.py:93
  45.9 24.6 %copy-start.4 = (s32[384]{0:T(512)}, s32[384]{0:T(512)S(1)}, u32[]{:S(2)}) copy-start(s32[384]{0:T(512)S(1)} %add.112) | copy-start | bytes 4612
  46.0 24.5 %copy-start.5 = (pred[384]{0:T(512)(128)(4,1)}, pred[384]{0:T(512)(128)(4,1)S(1)}, u32[]{:S(2)}) copy-start(pred[384]{0:T(512)(128)(4,1)S(1)} %lt.72) | copy-start | bytes 1156
  73.2 2.4 copy-start
  76.9 246.6 %reduce-scatter.4.cloned.1.call-start = ((), (), s32[]{:S(2)}) async-start(), calls=%async_computation.5 | async-start | bytes 30412800
Sparse Core Ops, SparseCore 0:
  77.0 68.1 all-gather.1
  168.3 155.1 reduce-scatter.3
where the time goes:
time: 333 us
  waiting for transfers between devices  149 us (45%)
  blocking collectives  79.9 us (24%)
  matrix products  33 us (10%)
  other arithmetic  23 us (7%)
  between operations  16.4 us (5%)
  local copies, waits for them, and re-layouts  16.2 us (5%)
  starting transfers between devices  15.3 us (5%)
    unnamed x3, waiting for transfers between devices  69.5 us
    all_gather x1, waiting for transfers between devices, body(): gathered = lax.all_gather(signed_rows, 'panel', axis=1, tiled=True)  68.3 us
    psum x1, blocking collectives, body(): right_hand = lax.psum(right_part, 'tm')  65.3 us
    dot_general x1, matrix products, body(): lax.dot_general(gathered, own_rows, (((0,), (0,)), ((), ())), preferred_e...  22.9 us
    all_to_all x1, blocking collectives, body(): lax.all_to_all(send_obs, 'tm', split_axis=0, concat_axis=0, tiled=True)  14.5 us
    all_to_all x1, waiting for transfers between devices, body(): lax.all_to_all(send_design, 'tm', split_axis=0, concat_axis=0, tiled=True)  9.49 us
    all_to_all x1, starting transfers between devices, body(): lax.all_to_all(send_params, 'tm', split_axis=0, concat_axis=0, tiled=True)  9.43 us
    gather x5, local copies, waits for them, and re-layouts, pick_rows(): return jnp.take(padded, source_row, axis=0)  7.16 us
  transfers between devices with their start and end apart: 4, of which 4 were waited for; matrix products, arithmetic and copies ran while one was open for 8% of the time, Pallas kernels for 0%

commit v1 on v0

--- a/solution.py
+++ b/solution.py
@@ -90,7 +90,9 @@
     right_hand = lax.psum(right_part, "tm")
     own_rows = jnp.concatenate([design_bf, terms_bf], axis=0)
     signed_rows = jnp.concatenate([design_bf, -terms_bf], axis=0)
-    gathered = lax.all_gather(signed_rows, "panel", axis=1, tiled=True)
+    then = lax.axis_size("panel")
+    e_now = jnp.concatenate([signed_rows] * then, axis=1)
+    gathered = lax.all_to_all(e_now, split_axis=1, tiled=True, axis_name="panel", concat_axis=1)
     product = lax.dot_general(
         gathered, own_rows, (((0,), (0,)), ((), ())), preferred_element_type=jnp.float32
     )

time: 333 us -> 396 us (1.19)
  blocking collectives: 79.9 us -> 158 us
  waiting for transfers between devices: 149 us -> 77.3 us
  other arithmetic: 23 us -> 71.9 us
  local copies, waits for them, and re-layouts: 16.2 us -> 20.4 us
    all_to_all x0 -> x1, blocking collectives: none -> 80.2 us  [body(): lax.all_to_all(e_now, split_axis=1, tiled=True, axis_name='panel', concat...]
    all_gather x1 -> x0, waiting for transfers between devices: 68.3 us -> none  [body(): gathered = lax.all_gather(signed_rows, 'panel', axis=1, tiled=True)]
    concatenate x1, other arithmetic: 1.31 us -> 49.4 us  [body(): e_now = jnp.concatenate([signed_rows] * then, axis=1)]
    unnamed x3 -> x2, waiting for transfers between devices: 69.5 us -> 67.7 us
  transfers between devices with their start and end apart: 4 -> 3, of which waited for: 4 -> 2; matrix products, arithmetic and copies ran while one was open for 8% -> 7% of each run, Pallas kernels for 0% -> 0%
where the time goes in v1:
time: 396 us; the launch traced here: 395 us
  blocking collectives  158 us (40%)
  waiting for transfers between devices  77.3 us (20%)
  other arithmetic  71.9 us (18%)
  matrix products  34 us (9%)
  local copies, waits for them, and re-layouts  20.4 us (5%)
  starting transfers between devices  16.9 us (4%)
  between operations  16.4 us (4%)
    all_to_all x1, blocking collectives, body(): lax.all_to_all(e_now, split_axis=1, tiled=True, axis_name='panel', concat...  80.2 us
    unnamed x2, waiting for transfers between devices  67.7 us
    psum x1, blocking collectives, body(): right_hand = lax.psum(right_part, 'tm')  65.3 us
    concatenate x1, other arithmetic, body(): e_now = jnp.concatenate([signed_rows] * then, axis=1)  49.4 us
    dot_general x1, matrix products, body(): lax.dot_general(gathered, own_rows, (((0,), (0,)), ((), ())), preferred_e...  26 us
    all_to_all x1, blocking collectives, body(): lax.all_to_all(send_obs, 'tm', split_axis=0, concat_axis=0, tiled=True)  12.9 us
    all_to_all x1, waiting for transfers between devices, body(): lax.all_to_all(send_design, 'tm', split_axis=0, concat_axis=0, tiled=True)  9.66 us
    all_to_all x1, starting transfers between devices, body(): lax.all_to_all(send_params, 'tm', split_axis=0, concat_axis=0, tiled=True)  9.43 us
  transfers between devices with their start and end apart: 3, of which 2 were waited for; matrix products, arithmetic and copies ran while one was open for 7% of the time, Pallas kernels for 0%

profile of v1, /device:TPU:1, one launch (start us, length us, event | category | flops | bytes accessed | tf_op | source)
XLA Modules:
  0.0 395.4 jit_solution(2891118962664698615)
XLA Ops:
  7.2 0.9 copy.22
  8.1 0.5 broadcast.193
  8.6 2.1 fusion.33
  10.7 0.1 reshape_squeeze.3
  10.8 0.0 copy-start.4
  10.8 0.2 dynamic-slice_reduce_fusion
  11.0 0.6 reduce-window.6
  11.6 0.2 slice_reduce_fusion
  11.8 0.1 fusion.36
  11.9 0.1 copy.21
  12.1 0.2 fusion.31
  12.3 1.4 scatter_custom_fusion
  13.7 0.7 pad_maximum_fusion
  14.5 2.8 gather_fusion.2
  17.3 0.1 broadcast_in_dim.54
  17.4 1.4 gather_fusion.1
  18.9 0.1 broadcast_select_fusion.1
  19.1 0.8 reshape.235
  19.8 9.4 %all-to-all-start.1 = ((bf16[32,2,384]{2,1,0:T(2,128)(2,1)}), bf16[32,2,384]{2,1,0:T(2,128)(2,1)S(1)}, u32[]{:S(2)}, u32[]{:S(2)}) async-start(bf16[32,2,384]{2,1,0:T(2,128)(2,1)} %reshape.235), calls=%async_computation.1 | async-start | bytes 98304 | tf_op jit(solution)/shard_map/all_to_all | solution.py:74
  29.3 0.7 and_select_fusion
  29.9 1.4 concatenate.18
  31.4 2.5 gather_fusion
  33.9 0.0 copy-start.8
  33.9 0.4 gather.17
  34.3 1.6 broadcast_select_fusion
  35.9 0.1 broadcast_add_fusion
  35.9 1.0 convert_reduce_fusion
  36.9 7.4 %all-to-all-start = ((bf16[32,12,1920]{2,1,0:T(8,128)(2,1)}), bf16[32,12,1920]{2,1,0:T(8,128)(2,1)S(1)}, u32[]{:S(2)}, u32[]{:S(2)}) async-start(bf16[32,12,1920]{2,1,0:T(8,128)(2,1)} %broadcast_select_fusion), calls=%async_computation | async-start | bytes 3932160 | tf_op jit(solution)/shard_map/all_to_all | solution.py:73
  44.3 0.0 reduce-scatter.4.cloned.1.call-start
  44.3 0.1 iota_compare_fusion.5
  44.4 0.6 dynamic_slice.10
  45.7 0.6 dynamic_slice.9
  47.6 0.1 add.112
  47.7 0.1 lt.72
  47.8 0.1 reshape.236
  48.0 0.7 fusion.27
  48.8 0.2 fusion.69
  49.0 0.1 copy.23
  49.1 5.8 %cholesky.17 = f32[64,64]{1,0:T(8,128)S(1)} custom-call(f32[64,64]{1,0:T(8,128)S(1)} %fusion.40), custom_call_target="Cholesky" | custom-call | tf_op jit(solution)/shard_map/jit(cholesky)/cholesky | solution.py:30
  55.0 0.6 compare_reduce_fusion
  55.6 0.7 fusion.32
  56.3 4.9 %custom-call.6 = f32[1,64,64]{1,2,0:T(8,128)S(1)} custom-call(f32[1,64,64]{2,1,0:T(8,128)S(1)} %fusion.32), custom_call_target="InvertDiagBlocksLowerTriangular" | custom-call | tf_op jit(solution)/shard_map/triangular_solve | solution.py:31
  61.2 0.3 fusion.37
  61.5 9.7 %all-to-all-done = bf16[32,12,1920]{2,1,0:T(8,128)(2,1)S(1)} async-done(((bf16[32,12,1920]{2,1,0:T(8,128)(2,1)}), bf16[32,12,1920]{2,1,0:T(8,128)(2,1)S(1)}, u32[]{:S(2)}, u32[]{:S(2)}) %all-to-all-start) | async-done | bytes 1474592 | tf_op jit(solution)/shard_map/all_to_all | solution.py:73
  71.2 0.4 reshape.167
  71.5 1.4 fusion.68
  73.0 1.7 fusion.67
  74.6 49.4 %maximum_maximum_fusion = bf16[448,7680]{1,0:T(8,128)(2,1)S(1)} fusion(bf16[64,1920]{1,0:T(8,128)(2,1)S(1)} %get-tuple-element.6, bf16[384,1920]{1,0:T(8,128)(2,1)S(1)} %get-tuple-element.9), kind=kLoop, calls=%fused_computation.6 | loop fusion | flops 55050240 | bytes 8601600 | tf_op jit(solution)/shard_map/concatenate | solution.py:94
  124.0 0.5 copy.32
  124.5 80.2 %all_to_all.28 = bf16[448,4,1920]{2,0,1:T(8,128)(2,1)S(1)} all-to-all(bf16[448,4,1920]{2,0,1:T(8,128)(2,1)S(1)} %bitcast.70), channel_id=1, replica_groups=mesh['tm'=32,'panel'=4] {'panel'}, dimensions={1} | all-to-all | bytes 13762560 | tf_op jit(solution)/shard_map/all_to_all | solution.py:95
  204.8 3.4 copy.29
  208.2 26.0 %multiply_convert_fusion = bf16[7680,1920]{1,0:T(8,128)(2,1)} fusion(bf16[448,7680]{1,0:T(8,128)(2,1)} %bitcast.72, bf16[64,1920]{1,0:T(8,128)(2,1)S(1)} %get-tuple-element.7, bf16[384,1920]{1,0:T(8,128)(2,1)S(1)} %copy-done.3), kind=kOutput, calls=%fused_computation.4 | convolution fusion | flops 13244989440 | bytes 38092800 | tf_op jit(solution)/shard_map/dot_general | solution.py:96
  234.2 0.0 reduce-scatter.4.cloned.1.call-update
  234.2 0.7 select_n.84
  235.0 12.9 %all_to_all.29 = bf16[32,1,12]{2,1,0:T(2,128)(2,1)S(1)} all-to-all(bf16[32,1,12]{2,1,0:T(2,128)(2,1)} %select_n.84), channel_id=1, replica_groups=mesh['tm'=32,'panel'=4] {'tm'}, dimensions={0} | all-to-all | bytes 1536 | tf_op jit(solution)/shard_map/all_to_all | solution.py:75
  247.8 0.7 reduce.12
  248.5 0.8 reshape.205
  249.3 1.4 convolution_bitcast_fusion
  250.7 0.2 convolution_bitcast_fusion.1
  250.9 0.4 convolution_reduce_fusion
  251.4 1.7 fusion.5
  253.0 65.3 %psum.7 = f32[1920]{0:T(1024)} all-reduce(f32[1920]{0:T(1024)S(1)} %subtract_multiply_fusion), channel_id=1, replica_groups=mesh['tm'=32,'panel'=4] {'tm'}, use_global_device_ids=true, to_apply=%region_9.10 | all-reduce | flops 1920 | bytes 15360 | tf_op jit(solution)/shard_map/psum | solution.py:90
  318.4 67.7 %reduce-scatter.4.cloned.1.call-done = bf16[240,1920]{1,0:T(8,128)(2,1)} async-done(((bf16[7680,1920]{1,0:T(8,128)(2,1)}), bf16[240,1920]{1,0:T(8,128)(2,1)}) %reduce-scatter.4.cloned.1.call-update) | async-done | bytes 921616
  386.0 2.5 convert_element_type.57
  (31 shorter events, 0.3 us)
Async XLA Ops:
  10.8 2.9 copy-start.4
  19.8 17.1 %all-to-all-start.1 = ((bf16[32,2,384]{2,1,0:T(2,128)(2,1)}), bf16[32,2,384]{2,1,0:T(2,128)(2,1)S(1)}, u32[]{:S(2)}, u32[]{:S(2)}) async-start(bf16[32,2,384]{2,1,0:T(2,128)(2,1)} %reshape.235), calls=%async_computation.1 | async-start | bytes 98304 | tf_op jit(solution)/shard_map/all_to_all | solution.py:74
  33.9 10.5 %copy-start.7 = (f32[32]{0:T(128)S(1)}, f32[32]{0:T(128)}, u32[]{:S(2)}) copy-start(f32[32]{0:T(128)} %param.11) | copy-start | bytes 388
  33.9 11.8 %copy-start.8 = (f32[32]{0:T(128)S(1)}, f32[32]{0:T(128)}, u32[]{:S(2)}) copy-start(f32[32]{0:T(128)} %param.10) | copy-start | bytes 388
  36.9 34.3 %all-to-all-start = ((bf16[32,12,1920]{2,1,0:T(8,128)(2,1)}), bf16[32,12,1920]{2,1,0:T(8,128)(2,1)S(1)}, u32[]{:S(2)}, u32[]{:S(2)}) async-start(bf16[32,12,1920]{2,1,0:T(8,128)(2,1)} %broadcast_select_fusion), calls=%async_computation | async-start | bytes 3932160 | tf_op jit(solution)/shard_map/all_to_all | solution.py:73
  44.3 341.7 %reduce-scatter.4.cloned.1.call-start = ((), (), s32[]{:S(2)}) async-start(), calls=%async_computation.5 | async-start | bytes 30412800
  47.7 25.2 %copy-start.5 = (s32[384]{0:T(512)}, s32[384]{0:T(512)S(1)}, u32[]{:S(2)}) copy-start(s32[384]{0:T(512)S(1)} %add.112) | copy-start | bytes 4612
  47.8 25.1 %copy-start.6 = (pred[384]{0:T(512)(128)(4,1)}, pred[384]{0:T(512)(128)(4,1)S(1)}, u32[]{:S(2)}) copy-start(pred[384]{0:T(512)(128)(4,1)S(1)} %lt.72) | copy-start | bytes 1156
  72.9 1.7 copy-start
  72.9 51.0 %copy-start.2 = (bf16[384,1920]{1,0:T(8,128)(2,1)}, bf16[384,1920]{1,0:T(8,128)(2,1)S(1)}, u32[]{:S(2)}) copy-start(bf16[384,1920]{1,0:T(8,128)(2,1)S(1)} %get-tuple-element.9) | copy-start | bytes 4423684
  204.8 3.4 copy-start.3
  234.2 17.1 %copy-start.1 = (f32[384,1920]{1,0:T(8,128)S(1)}, f32[384,1920]{1,0:T(8,128)}, u32[]{:S(2)}) copy-start(f32[384,1920]{1,0:T(8,128)} %copy-done) | copy-start | bytes 8847364
Sparse Core Ops, SparseCore 0:
  234.4 151.6 reduce-scatter.3
